TPU v7x, 128 devices: a whole 4x4x4 slice. The times are simulated.
128 devices in a mesh: corpus: 32 (over y, z, core), query: 4 (over x).
Axes of the slice: x: 4, y: 4, z: 4, core: 2. Of those that a mesh axis runs over, the one named last changes fastest.
Arguments:
- queries: bfloat16 [32768, 768], P(('corpus', 'query')), may hold values from -8 to 8
- probes: int32 [32768, 4], P(('corpus', 'query')), may hold values from 0 to 1023, as said below
- targets: int32 [32768, 8], P(('corpus', 'query')), may hold values from 0 to 4095, all different within a row
- passage_codes: int32 [1024, 96, 1024], P('corpus'), may hold values from 0 to 15
- codebook: float32 [16, 768], replicated, may hold values from -6 to 6
Outputs:
- grad_queries: bfloat16 [32768, 768], P(('corpus', 'query'))
- codebook_step: float32 [16, 768], replicated
Inputs may be any that keep to these rules, and one draw needn't show every extreme that they name: `probes`: each row names 4 different lists; list l belongs to index l // 32 of corpus. In every aligned block of 256 rows (the rows of one device) no list is named more than 2 times, and one list, the same one in every block, is named exactly 2 times. `targets`: each row names 8 different candidates; column r holds the candidate of rank r.
All inputs are finite; a program needn't handle non-finite values.
Results may differ from a plain program's by a relative error of at most 0.01.
The roundings to bfloat16 on the way count: a program that leaves them out, or rounds other values in their place, can miss the bound.
Values may be sent and summed in bfloat16 or wider, within the bound.
No kernel may reach another device: no remote copies, remote signals or barrier semaphores. Data moves between devices by JAX's collectives and lax.ppermute only.
A program may use at most 192 MiB of HBM per device.

v0:
```python
import jax
import jax.numpy as jnp
from jax import lax
from jax.sharding import PartitionSpec as P

D = 768
SUBSPACES = 96
CENTROIDS = 16
SUBDIM = 8
PASSAGES = 1024
PROBES = 4
TARGETS = 8
NEGATIVE = -1e30
EPSILON = 1e-06


def rank_weights():
    levels = jnp.arange(TARGETS, dtype=jnp.int32).astype(jnp.float32)
    return 2.0 * (TARGETS - levels) / (TARGETS * (TARGETS + 1.0))


def rank_slots(list_keys, key_count, keep):
    key_ids = jnp.arange(key_count, dtype=jnp.int32)
    marked = ((list_keys[:, None] == key_ids[None, :]) & keep[:, None]).astype(jnp.int32)
    running = jnp.cumsum(marked, axis=0)
    return jnp.sum(marked * running, axis=1) - 1


def note_block(probes, targets):
    row_count = probes.shape[0]
    probe_cols = jnp.arange(PROBES, dtype=jnp.int32)
    inside = targets[:, None, :] // PASSAGES == probe_cols[None, :, None]
    target_spot = jnp.where(inside, targets[:, None, :] % PASSAGES, -1)
    query_ids = jnp.broadcast_to(
        jnp.arange(row_count, dtype=jnp.int32)[:, None, None], (row_count, PROBES, 1)
    )
    return jnp.concatenate([query_ids, target_spot], axis=2).reshape(
        row_count * PROBES, TARGETS + 1
    )


def lookup_rows(rows_block, codebook):
    lead_shape = rows_block.shape[:-1]
    split_rows = rows_block.astype(jnp.float32).reshape(lead_shape + (SUBSPACES, SUBDIM))
    centroids = codebook.reshape(CENTROIDS, SUBSPACES, SUBDIM)
    lut_rows = jnp.einsum(
        "...me,kme->...mk", split_rows, centroids, precision=lax.Precision.HIGHEST
    )
    return lut_rows.reshape(lead_shape + (SUBSPACES * CENTROIDS,)).astype(jnp.bfloat16)


def code_one_hot(code_block):
    levels = jnp.arange(CENTROIDS, dtype=jnp.int32)
    marked = code_block[:, :, None, :] == levels[None, None, :, None]
    return marked.astype(jnp.bfloat16).reshape(
        code_block.shape[0], SUBSPACES * CENTROIDS, code_block.shape[2]
    )


def group_size(lists_dev, slot_rows):
    group_width = 1
    while (
        group_width * 2 <= lists_dev
        and lists_dev % (group_width * 2) == 0
        and (group_width * slot_rows < 512)
    ):
        group_width = group_width * 2
    return group_width


def first_pass(got_rows, passage_codes, codebook, group_width):
    lists_dev, slot_rows = (got_rows.shape[0], got_rows.shape[1])
    groups = lists_dev // group_width

    def score_piece(pieces):
        row_group, code_group = pieces
        lut_rows = lookup_rows(row_group, codebook)
        one_hot = code_one_hot(code_group)
        scores = jnp.einsum("grk,gkl->grl", lut_rows, one_hot, preferred_element_type=jnp.float32)
        top_score = jnp.max(scores, axis=2)
        exp_total = jnp.sum(jnp.exp(scores - top_score[:, :, None]), axis=2)
        return (scores, top_score, exp_total)

    scores, top_score, exp_total = lax.map(
        score_piece,
        (
            got_rows.reshape(groups, group_width, slot_rows, D),
            passage_codes.reshape(groups, group_width, SUBSPACES, PASSAGES),
        ),
    )
    return (
        scores.reshape(lists_dev, slot_rows, PASSAGES),
        top_score.reshape(lists_dev, slot_rows),
        exp_total.reshape(lists_dev, slot_rows),
    )


def second_pass(
    got_rows, got_notes, passage_codes, codebook, scores, query_top, query_total, group_width
):
    lists_dev, slot_rows = (got_rows.shape[0], got_rows.shape[1])
    groups = lists_dev // group_width
    weights = rank_weights()
    places = jnp.arange(PASSAGES, dtype=jnp.int32)
    centroids = codebook.reshape(CENTROIDS, SUBSPACES, SUBDIM)
    highest = lax.Precision.HIGHEST

    def grad_piece(pieces):
        row_group, note_group, code_group, score_group, top_group, total_group = pieces
        one_hot = code_one_hot(code_group)
        target_spot = note_group[:, :, 1:]
        teacher = jnp.sum(
            jnp.where(target_spot[:, :, :, None] == places, weights[:, None], 0.0), axis=2
        )
        student = jnp.exp(score_group - top_group[:, :, None]) / total_group[:, :, None]
        is_valid = note_group[:, :, 0] >= 0
        grad_scores = jnp.where(is_valid[:, :, None], student - teacher, 0.0).astype(jnp.bfloat16)
        histogram = jnp.einsum(
            "grl,gkl->grk", grad_scores, one_hot, preferred_element_type=jnp.float32
        )
        histogram = histogram.reshape(group_width, slot_rows, SUBSPACES, CENTROIDS)
        partial_value = jnp.einsum("grmk,kme->grme", histogram, centroids, precision=highest)
        split_rows = row_group.astype(jnp.float32).reshape(
            group_width, slot_rows, SUBSPACES, SUBDIM
        )
        book_part = jnp.einsum("grmk,grme->kme", histogram, split_rows, precision=highest)
        return (partial_value.reshape(group_width, slot_rows, D), book_part)

    partial_value, book_part = lax.map(
        grad_piece,
        (
            got_rows.reshape(groups, group_width, slot_rows, D),
            got_notes.reshape(groups, group_width, slot_rows, TARGETS + 1),
            passage_codes.reshape(groups, group_width, SUBSPACES, PASSAGES),
            scores.reshape(groups, group_width, slot_rows, PASSAGES),
            query_top.reshape(groups, group_width, slot_rows),
            query_total.reshape(groups, group_width, slot_rows),
        ),
    )
    return (
        partial_value.reshape(lists_dev, slot_rows, D),
        jnp.sum(book_part, axis=0).reshape(CENTROIDS, D),
    )


def shards(queries, probes, targets, passage_codes, codebook):
    corpus_size = lax.axis_size("corpus")
    query_rows = queries.shape[0]
    lists_dev = passage_codes.shape[0]
    list_total = lists_dev * corpus_size
    capacity = min(query_rows, max(2, 2 * PROBES * query_rows // list_total))
    slot_rows = corpus_size * capacity
    slot_count = lists_dev * slot_rows
    group_width = group_size(lists_dev, slot_rows)
    flat_probes = probes.reshape(-1)
    local_list = flat_probes % lists_dev
    owner_ids = flat_probes // lists_dev
    slot_rank = rank_slots(flat_probes, list_total, jnp.ones(flat_probes.shape, jnp.bool_))
    note_rows = note_block(probes, targets)
    placed = (local_list * corpus_size + owner_ids) * capacity + slot_rank
    sending = (
        jnp.zeros((slot_count, D), jnp.bfloat16).at[placed].set(jnp.repeat(queries, PROBES, axis=0))
    )
    note_buffer = jnp.full((slot_count, TARGETS + 1), -1, jnp.int32).at[placed].set(note_rows)
    got_rows, got_notes = (
        lax.all_to_all(
            sending.reshape(lists_dev, corpus_size, capacity, D),
            "corpus",
            split_axis=1,
            concat_axis=1,
            tiled=True,
        ),
        lax.all_to_all(
            note_buffer.reshape(lists_dev, corpus_size, capacity, TARGETS + 1),
            "corpus",
            split_axis=1,
            concat_axis=1,
            tiled=True,
        ),
    )
    got_rows = got_rows.reshape(lists_dev, slot_rows, D)
    got_notes = got_notes.reshape(lists_dev, slot_rows, TARGETS + 1)
    is_valid = got_notes[:, :, 0] >= 0
    scores, top_score, exp_total = first_pass(got_rows, passage_codes, codebook, group_width)
    top_score = jnp.where(is_valid, top_score, NEGATIVE)
    exp_total = jnp.where(is_valid, exp_total, 0.0)
    back_top, back_total = (
        lax.all_to_all(
            top_score.reshape(lists_dev, corpus_size, capacity),
            "corpus",
            split_axis=1,
            concat_axis=1,
            tiled=True,
        ),
        lax.all_to_all(
            exp_total.reshape(lists_dev, corpus_size, capacity),
            "corpus",
            split_axis=1,
            concat_axis=1,
            tiled=True,
        ),
    )
    entry_top = back_top.reshape(-1)[placed].reshape(query_rows, PROBES)
    entry_total = back_total.reshape(-1)[placed].reshape(query_rows, PROBES)
    own_top = jnp.max(entry_top, axis=1)
    own_total = jnp.sum(entry_total * jnp.exp(entry_top - own_top[:, None]), axis=1)
    slot_top = jnp.zeros((slot_count,), jnp.float32).at[placed].set(jnp.repeat(own_top, PROBES))
    slot_total = jnp.ones((slot_count,), jnp.float32).at[placed].set(jnp.repeat(own_total, PROBES))
    query_top, query_total = (
        lax.all_to_all(
            slot_top.reshape(lists_dev, corpus_size, capacity),
            "corpus",
            split_axis=1,
            concat_axis=1,
            tiled=True,
        ),
        lax.all_to_all(
            slot_total.reshape(lists_dev, corpus_size, capacity),
            "corpus",
            split_axis=1,
            concat_axis=1,
            tiled=True,
        ),
    )
    query_top = query_top.reshape(lists_dev, slot_rows)
    query_total = query_total.reshape(lists_dev, slot_rows)
    query_top = jnp.where(is_valid, query_top, 0.0)
    query_total = jnp.where(is_valid, query_total, 1.0)
    partial_value, book_part = second_pass(
        got_rows, got_notes, passage_codes, codebook, scores, query_top, query_total, group_width
    )
    returned = lax.all_to_all(
        partial_value.reshape(lists_dev, corpus_size, capacity, D),
        "corpus",
        split_axis=1,
        concat_axis=1,
        tiled=True,
    )
    per_probe = returned.reshape(slot_count, D)[placed].reshape(query_rows, PROBES, D)
    grad_queries = jnp.sum(per_probe, axis=1)
    book_sum = lax.psum(book_part, ("corpus", "query"))
    normed = book_sum * lax.rsqrt(jnp.mean(book_sum * book_sum) + EPSILON)
    return (grad_queries.astype(jnp.bfloat16), normed)


def solution(mesh):
    placed = (
        P(("corpus", "query"), None),
        P(("corpus", "query"), None),
        P(("corpus", "query"), None),
        P("corpus", None, None),
        P(),
    )
    return jax.shard_map(
        shards,
        mesh=mesh,
        in_specs=placed,
        out_specs=(P(("corpus", "query"), None), P()),
        check_vma=False,
    )
```

profile of v0, /device:TPU:1, one launch (start us, length us, event | category | flops | bytes accessed | tf_op | source)
XLA Modules:
  0.0 697.2 jit_solution(16750538512104853884)
XLA Ops:
  4.4 2.6 broadcast_add_fusion
  7.0 2.4 copy.130
  11.3 3.6 scatter_custom_fusion
  16.7 9.6 %all-to-all-start = ((s32[32,1,576]{2,1,0:T(1,128)}), s32[32,1,576]{2,1,0:T(1,128)S(1)}, u32[]{:S(2)}, u32[]{:S(2)}) async-start(s32[32,1,576]{2,1,0:T(1,128)} %reshape.393), calls=%async_computation | async-start | bytes 163840 | tf_op jit(solution)/shard_map/all_to_all | solution.py:173
  28.1 7.1 %scatter_custom_fusion.1 = bf16[2048,768]{1,0:T(8,128)(2,1)S(1)} fusion(s32[1024]{0:T(1024)S(1)} %bitcast.179, bf16[1024,768]{1,0:T(8,128)(2,1)} %reshape.360, bf16[]{:T(256)} %constant.118.clone.1), kind=kCustom, calls=%fused_computation.62 | custom fusion | bytes 3146240 | tf_op jit(solution)/shard_map/scatter | solution.py:162
  35.1 2.7 reshape.305
  37.9 6.8 copy.136
  44.7 7.4 %all-to-all-start.1 = ((bf16[32,32,2,768]{3,2,0,1:T(2,128)(2,1)}), bf16[32,32,2,768]{3,2,0,1:T(2,128)(2,1)S(1)}, u32[]{:S(2)}, u32[]{:S(2)}) async-start(bf16[32,32,2,768]{3,2,0,1:T(2,128)(2,1)} %copy.136), calls=%async_computation.1 | async-start | bytes 6291456 | tf_op jit(solution)/shard_map/all_to_all | solution.py:166
  60.2 31.6 %all-to-all-done.1 = bf16[32,32,2,768]{3,2,0,1:T(2,128)(2,1)S(1)} async-done(((bf16[32,32,2,768]{3,2,0,1:T(2,128)(2,1)}), bf16[32,32,2,768]{3,2,0,1:T(2,128)(2,1)S(1)}, u32[]{:S(2)}, u32[]{:S(2)}) %all-to-all-start.1) | async-done | bytes 3145760 | tf_op jit(solution)/shard_map/all_to_all | solution.py:166
  94.2 7.3 %copy.138 = bf16[4,8,64,768]{2,3,1,0:T(8,128)(2,1)} copy(bf16[4,8,64,768]{3,1,0,2:T(8,128)(2,1)} %bitcast.169) | data formatting | bytes 6291456 | tf_op jit(solution)/shard_map/while | solution.py:84
  102.7 129.6 %while.27 = (s32[]{:T(128)}, f32[4,8,64,1024]{3,2,1,0:T(8,128)}, f32[4,8,64]{2,1,0:T(8,128)}, f32[4,8,64]{2,1,0:T(8,128)}, bf16[4,8,64,768]{2,3,1,0:T(8,128)(2,1...) while((s32[]{:T(128)}, f32[4,8,64,1024]{3,2,1,0:T(8,128)}, ...), condition=%wide.region_8.9_spmd, body=%wide.region_5.8_spmd.sunk | while | flops 1701051392 | bytes 57241216 | solution.py:84
  102.7 4.1 convert_bitcast_fusion.2
  112.8 9.4 %bitcast_compare_fusion.4 = pred[8,1536,1024]{2,1,0:T(32,128)(4,1)} fusion(s32[1536]{0:T(1024)S(1)} %eq.177, s32[8,96,1024]{2,1,0:T(8,128)S(1)} %dynamic-slice_bitcast_fusion.14), kind=kLoop, calls=%fused_computation.9.clone.1 | loop fusion | flops 12582912 | bytes 15734784 | tf_op jit(solution)/shard_map/while/body/eval_jaxpr/eq | solution.py:54
  122.1 11.7 %bitcast_dynamic-update-slice_fusion.5 = (f32[4,8,64,1024]{3,2,1,0:T(8,128)}, f32[8,64,1024]{2,1,0:T(8,128)S(1)}) fusion(f32[4,8,64,1024]{3,2,1,0:T(8,128)} %get-tuple-element.387, s32[]{:T(128)} %get-tuple-element.386, bf16[8,64,1536]{1,2,0:T(8,128)(2,1)S(1)} %bitcast.165, pred[8,1536,1024]{2,1,0:T(32,128)(4,1)} %bitcast_compare_fusion.4), kind=kOutput, calls=%fused_computation.12.clone.1 | convolution fusion | flops 1610612736 | bytes 18350592 | tf_op jit(solution)/shard_map/while/body/eval_jaxpr/grk,gkl->grl/dot_general | solution.py:79
  135.1 4.1 convert_bitcast_fusion.2
  145.2 9.4 %bitcast_compare_fusion.4 = pred[8,1536,1024]{2,1,0:T(32,128)(4,1)} fusion(s32[1536]{0:T(1024)S(1)} %eq.177, s32[8,96,1024]{2,1,0:T(8,128)S(1)} %dynamic-slice_bitcast_fusion.14), kind=kLoop, calls=%fused_computation.9.clone.1 | loop fusion | flops 12582912 | bytes 15734784 | tf_op jit(solution)/shard_map/while/body/eval_jaxpr/eq | solution.py:54
  154.5 11.7 %bitcast_dynamic-update-slice_fusion.5 = (f32[4,8,64,1024]{3,2,1,0:T(8,128)}, f32[8,64,1024]{2,1,0:T(8,128)S(1)}) fusion(f32[4,8,64,1024]{3,2,1,0:T(8,128)} %get-tuple-element.387, s32[]{:T(128)} %get-tuple-element.386, bf16[8,64,1536]{1,2,0:T(8,128)(2,1)S(1)} %bitcast.165, pred[8,1536,1024]{2,1,0:T(32,128)(4,1)} %bitcast_compare_fusion.4), kind=kOutput, calls=%fused_computation.12.clone.1 | convolution fusion | flops 1610612736 | bytes 18350592 | tf_op jit(solution)/shard_map/while/body/eval_jaxpr/grk,gkl->grl/dot_general | solution.py:79
  167.5 4.1 convert_bitcast_fusion.2
  177.6 9.4 %bitcast_compare_fusion.4 = pred[8,1536,1024]{2,1,0:T(32,128)(4,1)} fusion(s32[1536]{0:T(1024)S(1)} %eq.177, s32[8,96,1024]{2,1,0:T(8,128)S(1)} %dynamic-slice_bitcast_fusion.14), kind=kLoop, calls=%fused_computation.9.clone.1 | loop fusion | flops 12582912 | bytes 15734784 | tf_op jit(solution)/shard_map/while/body/eval_jaxpr/eq | solution.py:54
  186.9 11.7 %bitcast_dynamic-update-slice_fusion.5 = (f32[4,8,64,1024]{3,2,1,0:T(8,128)}, f32[8,64,1024]{2,1,0:T(8,128)S(1)}) fusion(f32[4,8,64,1024]{3,2,1,0:T(8,128)} %get-tuple-element.387, s32[]{:T(128)} %get-tuple-element.386, bf16[8,64,1536]{1,2,0:T(8,128)(2,1)S(1)} %bitcast.165, pred[8,1536,1024]{2,1,0:T(32,128)(4,1)} %bitcast_compare_fusion.4), kind=kOutput, calls=%fused_computation.12.clone.1 | convolution fusion | flops 1610612736 | bytes 18350592 | tf_op jit(solution)/shard_map/while/body/eval_jaxpr/grk,gkl->grl/dot_general | solution.py:79
  199.9 4.1 convert_bitcast_fusion.2
  210.0 9.4 %bitcast_compare_fusion.4 = pred[8,1536,1024]{2,1,0:T(32,128)(4,1)} fusion(s32[1536]{0:T(1024)S(1)} %eq.177, s32[8,96,1024]{2,1,0:T(8,128)S(1)} %dynamic-slice_bitcast_fusion.14), kind=kLoop, calls=%fused_computation.9.clone.1 | loop fusion | flops 12582912 | bytes 15734784 | tf_op jit(solution)/shard_map/while/body/eval_jaxpr/eq | solution.py:54
  219.4 11.7 %bitcast_dynamic-update-slice_fusion.5 = (f32[4,8,64,1024]{3,2,1,0:T(8,128)}, f32[8,64,1024]{2,1,0:T(8,128)S(1)}) fusion(f32[4,8,64,1024]{3,2,1,0:T(8,128)} %get-tuple-element.387, s32[]{:T(128)} %get-tuple-element.386, bf16[8,64,1536]{1,2,0:T(8,128)(2,1)S(1)} %bitcast.165, pred[8,1536,1024]{2,1,0:T(32,128)(4,1)} %bitcast_compare_fusion.4), kind=kOutput, calls=%fused_computation.12.clone.1 | convolution fusion | flops 1610612736 | bytes 18350592 | tf_op jit(solution)/shard_map/while/body/eval_jaxpr/grk,gkl->grl/dot_general | solution.py:79
  235.6 11.5 %all_to_all.35 = f32[32,32,2]{0,2,1:T(2,128)S(1)} all-to-all(f32[32,32,2]{0,2,1:T(2,128)S(1)} %get-tuple-element.256), channel_id=1, replica_groups=mesh['corpus'=32,'query'=4] {'corpus'}, dimensions={1} | all-to-all | bytes 16384 | tf_op jit(solution)/shard_map/all_to_all | solution.py:188
  247.1 4.4 all-to-all-start.4
  253.0 6.2 gather_fusion
  260.2 6.2 gather_fusion.1
  266.9 4.5 scatter_custom_fusion.3
  272.8 7.5 %all-to-all-start.5 = ((f32[32,32,2]{0,2,1:T(2,128)}), f32[32,32,2]{0,2,1:T(2,128)S(1)}, u32[]{:S(2)}, u32[]{:S(2)}) async-start(f32[32,32,2]{0,2,1:T(2,128)} %copy.148), calls=%async_computation.5 | async-start | bytes 65536 | tf_op jit(solution)/shard_map/all_to_all | solution.py:217
  280.5 4.5 scatter_custom_fusion.2
  287.6 6.2 all-to-all-start.3
  295.2 5.9 all-to-all-done.3
  301.3 212.7 %while.28 = (s32[]{:T(128)}, f32[4,8,64,768]{3,1,0,2:T(8,128)}, f32[4,16,96,8]{1,3,2,0:T(8,128)}, s32[4,8,64,9]{2,1,3,0:T(8,128)S(1)}, f32[4,8,64,1024]{3,2,1,0:...) while((s32[]{:T(128)}, f32[4,8,64,768]{3,1,0,2:T(8,128)}, ...), condition=%wide.region_15.16_spmd.clone, body=%wide.region_13.15_spmd.clone.sunk | while | flops 1788871168 | bytes 67385192 | solution.py:129
  302.3 7.1 %select_reduce_fusion.2 = f32[8,64,1024]{2,1,0:T(8,128)} fusion(f32[8]{0:T(128)S(1)} %subtract_multiply_fusion.2, s32[8,64,8]{2,1,0:T(8,128)S(1)} %copy.183), kind=kLoop, calls=%fused_computation.21.clone.1 | loop fusion | flops 12058624 | bytes 2113568 | tf_op jit(solution)/shard_map/while/body/eval_jaxpr/reduce_sum | solution.py:112
  313.6 9.3 %bitcast_compare_fusion.5 = pred[8,1536,1024]{2,1,0:T(32,128)(4,1)} fusion(s32[1536]{0:T(1024)S(1)} %eq.184, s32[8,96,1024]{2,1,0:T(8,128)S(1)} %dynamic-slice_bitcast_fusion.15), kind=kLoop, calls=%fused_computation.19.clone.1 | loop fusion | flops 12582912 | bytes 15734784 | tf_op jit(solution)/shard_map/while/body/eval_jaxpr/eq | solution.py:54
  322.9 12.8 %fusion.84 = f32[8,64,1536]{1,2,0:T(8,128)} fusion(pred[8,1536,1024]{2,1,0:T(32,128)(4,1)} %bitcast_compare_fusion.5, f32[8,64,1024]{2,1,0:T(8,128)} %select_reduce_fusion.2, f32[4,8,64,1024]{3,2,1,0:T(8,128)} %get-tuple-element.430, s32[]{:T(128)} %get-tuple-element.415, f32[8,64]{1,0:T(8,128)S(1)} %get-tuple-element.375, ...), kind=kOutput, calls=%fused_computation.38.clone.1 | convolution fusion | flops 1613234176 | bytes 19928576 | tf_op jit(solution)/shard_map/while/body/eval_jaxpr/grl,gkl->grk/dot_general | solution.py:118
  335.8 5.5 fusion.85
  343.6 2.7 constant_dynamic-update-slice_fusion.2
  346.3 8.3 %fusion.86 = f32[4,16,96,8]{1,3,2,0:T(8,128)} fusion(f32[4,16,96,8]{1,3,2,0:T(8,128)} %get-tuple-element.417, s32[]{:T(128)} %get-tuple-element.415, f32[8,64,96,16]{1,3,2,0:T(8,128)} %bitcast.164, bf16[4,8,64,768]{2,3,1,0:T(8,128)(2,1)} %get-tuple-element.435), kind=kOutput, calls=%fused_computation.37.clone.1 | convolution fusion | flops 75497472 | bytes 8258560 | tf_op jit(solution)/shard_map/while/body/eval_jaxpr/grmk,grme->kme/dot_general | solution.py:126
  355.4 7.1 %select_reduce_fusion.2 = f32[8,64,1024]{2,1,0:T(8,128)} fusion(f32[8]{0:T(128)S(1)} %subtract_multiply_fusion.2, s32[8,64,8]{2,1,0:T(8,128)S(1)} %copy.183), kind=kLoop, calls=%fused_computation.21.clone.1 | loop fusion | flops 12058624 | bytes 2113568 | tf_op jit(solution)/shard_map/while/body/eval_jaxpr/reduce_sum | solution.py:112
  366.7 9.3 %bitcast_compare_fusion.5 = pred[8,1536,1024]{2,1,0:T(32,128)(4,1)} fusion(s32[1536]{0:T(1024)S(1)} %eq.184, s32[8,96,1024]{2,1,0:T(8,128)S(1)} %dynamic-slice_bitcast_fusion.15), kind=kLoop, calls=%fused_computation.19.clone.1 | loop fusion | flops 12582912 | bytes 15734784 | tf_op jit(solution)/shard_map/while/body/eval_jaxpr/eq | solution.py:54
  376.0 12.8 %fusion.84 = f32[8,64,1536]{1,2,0:T(8,128)} fusion(pred[8,1536,1024]{2,1,0:T(32,128)(4,1)} %bitcast_compare_fusion.5, f32[8,64,1024]{2,1,0:T(8,128)} %select_reduce_fusion.2, f32[4,8,64,1024]{3,2,1,0:T(8,128)} %get-tuple-element.430, s32[]{:T(128)} %get-tuple-element.415, f32[8,64]{1,0:T(8,128)S(1)} %get-tuple-element.375, ...), kind=kOutput, calls=%fused_computation.38.clone.1 | convolution fusion | flops 1613234176 | bytes 19928576 | tf_op jit(solution)/shard_map/while/body/eval_jaxpr/grl,gkl->grk/dot_general | solution.py:118
  388.9 5.5 fusion.85
  396.7 2.7 constant_dynamic-update-slice_fusion.2
  399.4 8.2 %fusion.86 = f32[4,16,96,8]{1,3,2,0:T(8,128)} fusion(f32[4,16,96,8]{1,3,2,0:T(8,128)} %get-tuple-element.417, s32[]{:T(128)} %get-tuple-element.415, f32[8,64,96,16]{1,3,2,0:T(8,128)} %bitcast.164, bf16[4,8,64,768]{2,3,1,0:T(8,128)(2,1)} %get-tuple-element.435), kind=kOutput, calls=%fused_computation.37.clone.1 | convolution fusion | flops 75497472 | bytes 8258560 | tf_op jit(solution)/shard_map/while/body/eval_jaxpr/grmk,grme->kme/dot_general | solution.py:126
  408.4 7.1 %select_reduce_fusion.2 = f32[8,64,1024]{2,1,0:T(8,128)} fusion(f32[8]{0:T(128)S(1)} %subtract_multiply_fusion.2, s32[8,64,8]{2,1,0:T(8,128)S(1)} %copy.183), kind=kLoop, calls=%fused_computation.21.clone.1 | loop fusion | flops 12058624 | bytes 2113568 | tf_op jit(solution)/shard_map/while/body/eval_jaxpr/reduce_sum | solution.py:112
  419.8 9.3 %bitcast_compare_fusion.5 = pred[8,1536,1024]{2,1,0:T(32,128)(4,1)} fusion(s32[1536]{0:T(1024)S(1)} %eq.184, s32[8,96,1024]{2,1,0:T(8,128)S(1)} %dynamic-slice_bitcast_fusion.15), kind=kLoop, calls=%fused_computation.19.clone.1 | loop fusion | flops 12582912 | bytes 15734784 | tf_op jit(solution)/shard_map/while/body/eval_jaxpr/eq | solution.py:54
  429.1 12.8 %fusion.84 = f32[8,64,1536]{1,2,0:T(8,128)} fusion(pred[8,1536,1024]{2,1,0:T(32,128)(4,1)} %bitcast_compare_fusion.5, f32[8,64,1024]{2,1,0:T(8,128)} %select_reduce_fusion.2, f32[4,8,64,1024]{3,2,1,0:T(8,128)} %get-tuple-element.430, s32[]{:T(128)} %get-tuple-element.415, f32[8,64]{1,0:T(8,128)S(1)} %get-tuple-element.375, ...), kind=kOutput, calls=%fused_computation.38.clone.1 | convolution fusion | flops 1613234176 | bytes 19928576 | tf_op jit(solution)/shard_map/while/body/eval_jaxpr/grl,gkl->grk/dot_general | solution.py:118
  441.9 5.5 fusion.85
  449.8 2.7 constant_dynamic-update-slice_fusion.2
  452.5 8.2 %fusion.86 = f32[4,16,96,8]{1,3,2,0:T(8,128)} fusion(f32[4,16,96,8]{1,3,2,0:T(8,128)} %get-tuple-element.417, s32[]{:T(128)} %get-tuple-element.415, f32[8,64,96,16]{1,3,2,0:T(8,128)} %bitcast.164, bf16[4,8,64,768]{2,3,1,0:T(8,128)(2,1)} %get-tuple-element.435), kind=kOutput, calls=%fused_computation.37.clone.1 | convolution fusion | flops 75497472 | bytes 8258560 | tf_op jit(solution)/shard_map/while/body/eval_jaxpr/grmk,grme->kme/dot_general | solution.py:126
  461.5 7.1 %select_reduce_fusion.2 = f32[8,64,1024]{2,1,0:T(8,128)} fusion(f32[8]{0:T(128)S(1)} %subtract_multiply_fusion.2, s32[8,64,8]{2,1,0:T(8,128)S(1)} %copy.183), kind=kLoop, calls=%fused_computation.21.clone.1 | loop fusion | flops 12058624 | bytes 2113568 | tf_op jit(solution)/shard_map/while/body/eval_jaxpr/reduce_sum | solution.py:112
  472.8 9.3 %bitcast_compare_fusion.5 = pred[8,1536,1024]{2,1,0:T(32,128)(4,1)} fusion(s32[1536]{0:T(1024)S(1)} %eq.184, s32[8,96,1024]{2,1,0:T(8,128)S(1)} %dynamic-slice_bitcast_fusion.15), kind=kLoop, calls=%fused_computation.19.clone.1 | loop fusion | flops 12582912 | bytes 15734784 | tf_op jit(solution)/shard_map/while/body/eval_jaxpr/eq | solution.py:54
  482.2 12.8 %fusion.84 = f32[8,64,1536]{1,2,0:T(8,128)} fusion(pred[8,1536,1024]{2,1,0:T(32,128)(4,1)} %bitcast_compare_fusion.5, f32[8,64,1024]{2,1,0:T(8,128)} %select_reduce_fusion.2, f32[4,8,64,1024]{3,2,1,0:T(8,128)} %get-tuple-element.430, s32[]{:T(128)} %get-tuple-element.415, f32[8,64]{1,0:T(8,128)S(1)} %get-tuple-element.375, ...), kind=kOutput, calls=%fused_computation.38.clone.1 | convolution fusion | flops 1613234176 | bytes 19928576 | tf_op jit(solution)/shard_map/while/body/eval_jaxpr/grl,gkl->grk/dot_general | solution.py:118
  495.0 5.5 fusion.85
  502.8 2.7 constant_dynamic-update-slice_fusion.2
  505.6 8.2 %fusion.86 = f32[4,16,96,8]{1,3,2,0:T(8,128)} fusion(f32[4,16,96,8]{1,3,2,0:T(8,128)} %get-tuple-element.417, s32[]{:T(128)} %get-tuple-element.415, f32[8,64,96,16]{1,3,2,0:T(8,128)} %bitcast.164, bf16[4,8,64,768]{2,3,1,0:T(8,128)(2,1)} %get-tuple-element.435), kind=kOutput, calls=%fused_computation.37.clone.1 | convolution fusion | flops 75497472 | bytes 8258560 | tf_op jit(solution)/shard_map/while/body/eval_jaxpr/grmk,grme->kme/dot_general | solution.py:126
  514.1 5.0 all-to-all-start.6
  519.2 141.8 %psum.7 = f32[16,768]{0,1:T(8,128)S(1)} all-reduce(f32[16,768]{0,1:T(8,128)S(1)} %bitcast.174), channel_id=1, replica_groups=mesh['corpus'=32,'query'=4] {'corpus','query'}, use_global_device_ids=true, to_apply=%region_18.19 | all-reduce | flops 12288 | bytes 98304 | tf_op jit(solution)/shard_map/psum | solution.py:241
  663.2 10.3 %copy.154 = f32[32,32,2,768]{3,2,1,0:T(2,128)} copy(f32[32,32,2,768]{3,0,2,1:T(8,128)} %all-to-all-done.6) | data formatting | bytes 12582912 | tf_op jit(solution)/shard_map/all_to_all | solution.py:232
  673.5 8.5 %reshape.321 = f32[2048,768]{1,0:T(8,128)} reshape(f32[32,32,2,768]{3,2,1,0:T(2,128)} %copy.154) | data formatting | bytes 12582912 | tf_op jit(solution)/shard_map/reshape | solution.py:239
  682.1 8.7 %gather_fusion.2 = f32[1024,768]{1,0:T(8,128)} fusion(f32[2048,768]{1,0:T(8,128)} %reshape.321, s32[1024]{0:T(1024)S(1)} %copy-done.14), kind=kCustom, calls=%fused_computation.2 | custom fusion | bytes 6295552 | tf_op jit(solution)/shard_map/gather | solution.py:239
  690.8 3.1 reshape.322
  693.9 2.9 reduce_sum.65
  (225 shorter events, 92.1 us)
Async XLA Ops:
  2.4 1.9 copy-start.1
  9.5 0.8 copy-start.16
  10.2 16.1 %copy-start.7 = (bf16[256,768]{1,0:T(8,128)(2,1)S(1)}, bf16[256,768]{1,0:T(8,128)(2,1)}, u32[]{:S(2)}) copy-start(bf16[256,768]{1,0:T(8,128)(2,1)} %param.9) | copy-start | bytes 1179652
  10.9 17.1 %copy-start.15 = (s32[1024,1]{0,1:T(1,128)}, s32[1024,1]{0,1:T(1,128)S(1)}, u32[]{:S(2)}) copy-start(s32[1024,1]{0,1:T(1,128)S(1)} %compare_select_fusion.1) | copy-start | bytes 12292
  16.7 28.0 %all-to-all-start = ((s32[32,1,576]{2,1,0:T(1,128)}), s32[32,1,576]{2,1,0:T(1,128)S(1)}, u32[]{:S(2)}, u32[]{:S(2)}) async-start(s32[32,1,576]{2,1,0:T(1,128)} %reshape.393), calls=%async_computation | async-start | bytes 163840 | tf_op jit(solution)/shard_map/all_to_all | solution.py:173
  44.7 7.4 %copy-start.8 = (s32[32,1,576]{2,1,0:T(1,128)}, s32[32,1,576]{2,1,0:T(1,128)S(1)}, u32[]{:S(2)}) copy-start(s32[32,1,576]{2,1,0:T(1,128)S(1)} %all-to-all-done) | copy-start | bytes 221188
  44.7 47.1 %all-to-all-start.1 = ((bf16[32,32,2,768]{3,2,0,1:T(2,128)(2,1)}), bf16[32,32,2,768]{3,2,0,1:T(2,128)(2,1)S(1)}, u32[]{:S(2)}, u32[]{:S(2)}) async-start(bf16[32,32,2,768]{3,2,0,1:T(2,128)(2,1)} %copy.136), calls=%async_computation.1 | async-start | bytes 6291456 | tf_op jit(solution)/shard_map/all_to_all | solution.py:166
  58.8 0.7 copy-start.3
  112.8 9.4 %copy-start = (bf16[8,64,96,16]{1,3,2,0:T(8,128)(2,1)S(1)}, bf16[8,64,96,16]{1,3,2,0:T(8,128)(2,1)}, u32[]{:S(2)}) copy-start(bf16[8,64,96,16]{1,3,2,0:T(8,128)(2,1)} %copy.181) | copy-start | bytes 4718596 | tf_op jit(solution)/shard_map/while
  145.2 9.4 %copy-start = (bf16[8,64,96,16]{1,3,2,0:T(8,128)(2,1)S(1)}, bf16[8,64,96,16]{1,3,2,0:T(8,128)(2,1)}, u32[]{:S(2)}) copy-start(bf16[8,64,96,16]{1,3,2,0:T(8,128)(2,1)} %copy.181) | copy-start | bytes 4718596 | tf_op jit(solution)/shard_map/while
  177.6 9.4 %copy-start = (bf16[8,64,96,16]{1,3,2,0:T(8,128)(2,1)S(1)}, bf16[8,64,96,16]{1,3,2,0:T(8,128)(2,1)}, u32[]{:S(2)}) copy-start(bf16[8,64,96,16]{1,3,2,0:T(8,128)(2,1)} %copy.181) | copy-start | bytes 4718596 | tf_op jit(solution)/shard_map/while
  210.0 9.4 %copy-start = (bf16[8,64,96,16]{1,3,2,0:T(8,128)(2,1)S(1)}, bf16[8,64,96,16]{1,3,2,0:T(8,128)(2,1)}, u32[]{:S(2)}) copy-start(bf16[8,64,96,16]{1,3,2,0:T(8,128)(2,1)} %copy.181) | copy-start | bytes 4718596 | tf_op jit(solution)/shard_map/while
  247.1 12.3 %all-to-all-start.4 = ((f32[32,32,2]{0,2,1:T(2,128)}), f32[32,32,2]{0,2,1:T(2,128)S(1)}, u32[]{:S(2)}, u32[]{:S(2)}) async-start(f32[32,32,2]{0,2,1:T(2,128)} %get-tuple-element.255), calls=%async_computation.4 | async-start | bytes 65536 | tf_op jit(solution)/shard_map/all_to_all | solution.py:195
  252.2 14.2 %copy-start.13 = (s32[1024]{0:T(1024)}, s32[1024]{0:T(1024)S(1)}, u32[]{:S(2)}) copy-start(s32[1024]{0:T(1024)S(1)} %broadcast_clamp_fusion) | copy-start | bytes 12292
  259.4 34.5 %copy-start.4 = (s32[32,32,2,9]{0,2,1,3:T(2,128)S(1)}, s32[32,32,2,9]{0,2,1,3:T(2,128)}, u32[]{:S(2)}) copy-start(s32[32,32,2,9]{0,2,1,3:T(2,128)} %copy-done.3) | copy-start | bytes 221188
  272.8 14.8 %all-to-all-start.5 = ((f32[32,32,2]{0,2,1:T(2,128)}), f32[32,32,2]{0,2,1:T(2,128)S(1)}, u32[]{:S(2)}, u32[]{:S(2)}) async-start(f32[32,32,2]{0,2,1:T(2,128)} %copy.148), calls=%async_computation.5 | async-start | bytes 65536 | tf_op jit(solution)/shard_map/all_to_all | solution.py:217
  287.6 13.5 %all-to-all-start.3 = ((f32[32,32,2]{0,2,1:T(2,128)}), f32[32,32,2]{0,2,1:T(2,128)S(1)}, u32[]{:S(2)}, u32[]{:S(2)}) async-start(f32[32,32,2]{0,2,1:T(2,128)} %copy.144), calls=%async_computation.3 | async-start | bytes 65536 | tf_op jit(solution)/shard_map/all_to_all | solution.py:210
  301.5 0.6 copy-start.9
  301.5 0.6 copy-start.11
  301.5 8.5 %copy-start.5 = (s32[4,8,64,9]{2,1,3,0:T(8,128)}, s32[4,8,64,9]{2,1,3,0:T(8,128)S(1)}, u32[]{:S(2)}) copy-start(s32[4,8,64,9]{2,1,3,0:T(8,128)S(1)} %get-tuple-element.429) | copy-start | bytes 221188 | tf_op jit(solution)/shard_map/while
  346.3 8.3 %copy-start.6 = (s32[4,8,64,9]{2,1,3,0:T(8,128)S(1)}, s32[4,8,64,9]{2,1,3,0:T(8,128)}, u32[]{:S(2)}) copy-start(s32[4,8,64,9]{2,1,3,0:T(8,128)} %copy-done.5) | copy-start | bytes 221188 | tf_op jit(solution)/shard_map/while
  346.3 8.3 %copy-start.10 = (f32[4,8,64]{2,1,0:T(8,128)S(1)}, f32[4,8,64]{2,1,0:T(8,128)}, u32[]{:S(2)}) copy-start(f32[4,8,64]{2,1,0:T(8,128)} %copy-done.9) | copy-start | bytes 24580 | tf_op jit(solution)/shard_map/while
  346.3 8.3 %copy-start.12 = (f32[4,8,64]{2,1,0:T(8,128)S(1)}, f32[4,8,64]{2,1,0:T(8,128)}, u32[]{:S(2)}) copy-start(f32[4,8,64]{2,1,0:T(8,128)} %copy-done.11) | copy-start | bytes 24580 | tf_op jit(solution)/shard_map/while
  354.6 0.6 copy-start.9
  354.6 0.6 copy-start.11
  354.6 8.5 %copy-start.5 = (s32[4,8,64,9]{2,1,3,0:T(8,128)}, s32[4,8,64,9]{2,1,3,0:T(8,128)S(1)}, u32[]{:S(2)}) copy-start(s32[4,8,64,9]{2,1,3,0:T(8,128)S(1)} %get-tuple-element.429) | copy-start | bytes 221188 | tf_op jit(solution)/shard_map/while
  399.4 8.2 %copy-start.6 = (s32[4,8,64,9]{2,1,3,0:T(8,128)S(1)}, s32[4,8,64,9]{2,1,3,0:T(8,128)}, u32[]{:S(2)}) copy-start(s32[4,8,64,9]{2,1,3,0:T(8,128)} %copy-done.5) | copy-start | bytes 221188 | tf_op jit(solution)/shard_map/while
  399.4 8.2 %copy-start.10 = (f32[4,8,64]{2,1,0:T(8,128)S(1)}, f32[4,8,64]{2,1,0:T(8,128)}, u32[]{:S(2)}) copy-start(f32[4,8,64]{2,1,0:T(8,128)} %copy-done.9) | copy-start | bytes 24580 | tf_op jit(solution)/shard_map/while
  399.4 8.2 %copy-start.12 = (f32[4,8,64]{2,1,0:T(8,128)S(1)}, f32[4,8,64]{2,1,0:T(8,128)}, u32[]{:S(2)}) copy-start(f32[4,8,64]{2,1,0:T(8,128)} %copy-done.11) | copy-start | bytes 24580 | tf_op jit(solution)/shard_map/while
  407.7 0.6 copy-start.9
  407.7 0.6 copy-start.11
  407.7 8.5 %copy-start.5 = (s32[4,8,64,9]{2,1,3,0:T(8,128)}, s32[4,8,64,9]{2,1,3,0:T(8,128)S(1)}, u32[]{:S(2)}) copy-start(s32[4,8,64,9]{2,1,3,0:T(8,128)S(1)} %get-tuple-element.429) | copy-start | bytes 221188 | tf_op jit(solution)/shard_map/while
  452.5 8.3 %copy-start.6 = (s32[4,8,64,9]{2,1,3,0:T(8,128)S(1)}, s32[4,8,64,9]{2,1,3,0:T(8,128)}, u32[]{:S(2)}) copy-start(s32[4,8,64,9]{2,1,3,0:T(8,128)} %copy-done.5) | copy-start | bytes 221188 | tf_op jit(solution)/shard_map/while
  452.5 8.3 %copy-start.10 = (f32[4,8,64]{2,1,0:T(8,128)S(1)}, f32[4,8,64]{2,1,0:T(8,128)}, u32[]{:S(2)}) copy-start(f32[4,8,64]{2,1,0:T(8,128)} %copy-done.9) | copy-start | bytes 24580 | tf_op jit(solution)/shard_map/while
  452.5 8.3 %copy-start.12 = (f32[4,8,64]{2,1,0:T(8,128)S(1)}, f32[4,8,64]{2,1,0:T(8,128)}, u32[]{:S(2)}) copy-start(f32[4,8,64]{2,1,0:T(8,128)} %copy-done.11) | copy-start | bytes 24580 | tf_op jit(solution)/shard_map/while
  460.7 0.6 copy-start.9
  460.8 0.6 copy-start.11
  460.8 8.5 %copy-start.5 = (s32[4,8,64,9]{2,1,3,0:T(8,128)}, s32[4,8,64,9]{2,1,3,0:T(8,128)S(1)}, u32[]{:S(2)}) copy-start(s32[4,8,64,9]{2,1,3,0:T(8,128)S(1)} %get-tuple-element.429) | copy-start | bytes 221188 | tf_op jit(solution)/shard_map/while
  505.6 8.2 %copy-start.6 = (s32[4,8,64,9]{2,1,3,0:T(8,128)S(1)}, s32[4,8,64,9]{2,1,3,0:T(8,128)}, u32[]{:S(2)}) copy-start(s32[4,8,64,9]{2,1,3,0:T(8,128)} %copy-done.5) | copy-start | bytes 221188 | tf_op jit(solution)/shard_map/while
  505.6 8.2 %copy-start.10 = (f32[4,8,64]{2,1,0:T(8,128)S(1)}, f32[4,8,64]{2,1,0:T(8,128)}, u32[]{:S(2)}) copy-start(f32[4,8,64]{2,1,0:T(8,128)} %copy-done.9) | copy-start | bytes 24580 | tf_op jit(solution)/shard_map/while
  505.6 8.2 %copy-start.12 = (f32[4,8,64]{2,1,0:T(8,128)S(1)}, f32[4,8,64]{2,1,0:T(8,128)}, u32[]{:S(2)}) copy-start(f32[4,8,64]{2,1,0:T(8,128)} %copy-done.11) | copy-start | bytes 24580 | tf_op jit(solution)/shard_map/while
  514.0 5.0 copy-start.2
  514.1 149.2 %all-to-all-start.6 = ((f32[32,32,2,768]{3,0,2,1:T(8,128)}), f32[32,32,2,768]{3,0,2,1:T(8,128)}, u32[]{:S(2)}, u32[]{:S(2)}) async-start(f32[32,32,2,768]{3,0,2,1:T(8,128)} %bitcast.170), calls=%async_computation.6 | async-start | bytes 12582912 | tf_op jit(solution)/shard_map/all_to_all | solution.py:232
  673.5 8.5 %copy-start.14 = (s32[1024]{0:T(1024)S(1)}, s32[1024]{0:T(1024)}, u32[]{:S(2)}) copy-start(s32[1024]{0:T(1024)} %copy-done.13) | copy-start | bytes 12292
where the time goes:
time: 708 us; the launch traced here: 697 us
  matrix products  170 us (24%)
  local copies, waits for them, and re-layouts  168 us (24%)
  blocking collectives  153 us (22%)
  other arithmetic  125 us (18%)
  starting transfers between devices  40.1 us (6%)
  waiting for transfers between devices  38.7 us (5%)
    psum x1, blocking collectives, shards(): book_sum = lax.psum(book_part, ('corpus', 'query'))  142 us
    eq x8, other arithmetic, code_one_hot(): marked = code_block[:, :, None, :] == levels[None, None, :, None]  74.8 us
    dot_general x4, matrix products, grad_piece(): jnp.einsum('grl,gkl->grk', grad_scores, one_hot, preferred_element_type=j...  51.3 us
    dot_general x4, matrix products, score_piece(): jnp.einsum('grk,gkl->grl', lut_rows, one_hot, preferred_element_type=jnp....  46.8 us
    dot_general x4, matrix products, grad_piece(): jnp.einsum('grmk,grme->kme', histogram, split_rows, precision=highest)  33 us
    all_to_all x1, waiting for transfers between devices, shards(): lax.all_to_all(sending.reshape(lists_dev, corpus_size, capacity, D), 'cor...  31.6 us
    eq x24, local copies, waits for them, and re-layouts, code_one_hot(): marked = code_block[:, :, None, :] == levels[None, None, :, None]  28.9 us
    reduce_sum x4, other arithmetic, grad_piece(): jnp.sum(jnp.where(target_spot[:, :, :, None] == places, weights[:, None],...  28.5 us
  transfers between devices with their start and end apart: 6, of which 3 were waited for; matrix products, arithmetic and copies ran while one was open for 6% of the time, Pallas kernels for 0%

commit v1 on v0

--- a/solution.py
+++ b/solution.py
@@ -238,7 +238,7 @@
     )
     per_probe = returned.reshape(slot_count, D)[placed].reshape(query_rows, PROBES, D)
     grad_queries = jnp.sum(per_probe, axis=1)
-    book_sum = lax.psum(book_part, ("corpus", "query"))
+    book_sum = jnp.sum(lax.all_gather(book_part, ("corpus", "query")), axis=0)
     normed = book_sum * lax.rsqrt(jnp.mean(book_sum * book_sum) + EPSILON)
     return (grad_queries.astype(jnp.bfloat16), normed)
 

time: 708 us -> 662 us (0.935)
  blocking collectives: 153 us -> 96.4 us
  between operations: 2.26 us -> 15.6 us
    psum x1 -> x0, blocking collectives: 142 us -> none  [shards(): book_sum = lax.psum(book_part, ('corpus', 'query'))]
    all_to_all x0 -> x1, blocking collectives: none -> 84.9 us  [shards(): lax.all_to_all(partial_value.reshape(lists_dev, corpus_size, capacity, D)...]
  transfers between devices with their start and end apart: 6 -> 6, of which waited for: 3 -> 3; matrix products, arithmetic and copies ran while one was open for 6% -> 11% of each run, Pallas kernels for 0% -> 0%
where the time goes in v1:
time: 662 us; the launch traced here: 651 us
  matrix products  170 us (26%)
  local copies, waits for them, and re-layouts  166 us (25%)
  other arithmetic  129 us (19%)
  blocking collectives  96.4 us (15%)
  waiting for transfers between devices  38.5 us (6%)
  starting transfers between devices  35.6 us (5%)
  between operations  15.6 us (2%)
    all_to_all x1, blocking collectives, shards(): lax.all_to_all(partial_value.reshape(lists_dev, corpus_size, capacity, D)...  84.9 us
    eq x8, other arithmetic, code_one_hot(): marked = code_block[:, :, None, :] == levels[None, None, :, None]  74.8 us
    dot_general x4, matrix products, grad_piece(): jnp.einsum('grl,gkl->grk', grad_scores, one_hot, preferred_element_type=j...  51.2 us
    dot_general x4, matrix products, score_piece(): jnp.einsum('grk,gkl->grl', lut_rows, one_hot, preferred_element_type=jnp....  46.8 us
    dot_general x4, matrix products, grad_piece(): jnp.einsum('grmk,grme->kme', histogram, split_rows, precision=highest)  33 us
    all_to_all x1, waiting for transfers between devices, shards(): lax.all_to_all(sending.reshape(lists_dev, corpus_size, capacity, D), 'cor...  31.4 us
    eq x24, local copies, waits for them, and re-layouts, code_one_hot(): marked = code_block[:, :, None, :] == levels[None, None, :, None]  28.9 us
    reduce_sum x4, other arithmetic, grad_piece(): jnp.sum(jnp.where(target_spot[:, :, :, None] == places, weights[:, None],...  28.5 us
  transfers between devices with their start and end apart: 6, of which 3 were waited for; matrix products, arithmetic and copies ran while one was open for 11% of the time, Pallas kernels for 0%

profile of v1, /device:TPU:1, one launch (start us, length us, event | category | flops | bytes accessed | tf_op | source)
XLA Modules:
  0.0 651.4 jit_solution(3782662700504887091)
XLA Ops:
  10.9 2.6 broadcast_add_fusion
  13.5 2.4 copy.130
  17.9 3.6 scatter_custom_fusion
  23.2 9.6 %all-to-all-start = ((s32[32,1,576]{2,1,0:T(1,128)}), s32[32,1,576]{2,1,0:T(1,128)S(1)}, u32[]{:S(2)}, u32[]{:S(2)}) async-start(s32[32,1,576]{2,1,0:T(1,128)} %reshape.389), calls=%async_computation | async-start | bytes 163840 | tf_op jit(solution)/shard_map/all_to_all | solution.py:173
  34.6 7.1 %scatter_custom_fusion.1 = bf16[2048,768]{1,0:T(8,128)(2,1)S(1)} fusion(s32[1024]{0:T(1024)S(1)} %bitcast.179, bf16[1024,768]{1,0:T(8,128)(2,1)} %reshape.356, bf16[]{:T(256)} %constant.118.clone.1), kind=kCustom, calls=%fused_computation.62 | custom fusion | bytes 3146240 | tf_op jit(solution)/shard_map/scatter | solution.py:162
  41.7 2.7 reshape.302
  44.4 6.8 %copy.136 = bf16[32,32,2,768]{3,2,0,1:T(2,128)(2,1)} copy(bf16[32,32,2,768]{3,2,1,0:T(2,128)(2,1)} %reshape.302) | data formatting | bytes 6291456 | tf_op jit(solution)/shard_map/reshape | solution.py:167
  51.2 7.7 %all-to-all-start.1 = ((bf16[32,32,2,768]{3,2,0,1:T(2,128)(2,1)}), bf16[32,32,2,768]{3,2,0,1:T(2,128)(2,1)S(1)}, u32[]{:S(2)}, u32[]{:S(2)}) async-start(bf16[32,32,2,768]{3,2,0,1:T(2,128)(2,1)} %copy.136), calls=%async_computation.1 | async-start | bytes 6291456 | tf_op jit(solution)/shard_map/all_to_all | solution.py:166
  67.1 31.4 %all-to-all-done.1 = bf16[32,32,2,768]{3,2,0,1:T(2,128)(2,1)S(1)} async-done(((bf16[32,32,2,768]{3,2,0,1:T(2,128)(2,1)}), bf16[32,32,2,768]{3,2,0,1:T(2,128)(2,1)S(1)}, u32[]{:S(2)}, u32[]{:S(2)}) %all-to-all-start.1) | async-done | bytes 3145760 | tf_op jit(solution)/shard_map/all_to_all | solution.py:166
  100.9 7.3 %copy.138 = bf16[4,8,64,768]{2,3,1,0:T(8,128)(2,1)} copy(bf16[4,8,64,768]{3,1,0,2:T(8,128)(2,1)} %bitcast.169) | data formatting | bytes 6291456 | tf_op jit(solution)/shard_map/while | solution.py:84
  109.4 129.6 %while.27 = (s32[]{:T(128)}, f32[4,8,64,1024]{3,2,1,0:T(8,128)}, f32[4,8,64]{2,1,0:T(8,128)}, f32[4,8,64]{2,1,0:T(8,128)}, bf16[4,8,64,768]{2,3,1,0:T(8,128)(2,1...) while((s32[]{:T(128)}, f32[4,8,64,1024]{3,2,1,0:T(8,128)}, ...), condition=%wide.region_8.9_spmd, body=%wide.region_5.8_spmd.sunk | while | flops 1701051392 | bytes 57241216 | solution.py:84
  109.4 4.1 convert_bitcast_fusion.2
  119.5 9.4 %bitcast_compare_fusion.4 = pred[8,1536,1024]{2,1,0:T(32,128)(4,1)} fusion(s32[1536]{0:T(1024)S(1)} %eq.177, s32[8,96,1024]{2,1,0:T(8,128)S(1)} %dynamic-slice_bitcast_fusion.14), kind=kLoop, calls=%fused_computation.9.clone.1 | loop fusion | flops 12582912 | bytes 15734784 | tf_op jit(solution)/shard_map/while/body/eval_jaxpr/eq | solution.py:54
  128.8 11.7 %bitcast_dynamic-update-slice_fusion.5 = (f32[4,8,64,1024]{3,2,1,0:T(8,128)}, f32[8,64,1024]{2,1,0:T(8,128)S(1)}) fusion(f32[4,8,64,1024]{3,2,1,0:T(8,128)} %get-tuple-element.383, s32[]{:T(128)} %get-tuple-element.382, bf16[8,64,1536]{1,2,0:T(8,128)(2,1)S(1)} %bitcast.165, pred[8,1536,1024]{2,1,0:T(32,128)(4,1)} %bitcast_compare_fusion.4), kind=kOutput, calls=%fused_computation.12.clone.1 | convolution fusion | flops 1610612736 | bytes 18350592 | tf_op jit(solution)/shard_map/while/body/eval_jaxpr/grk,gkl->grl/dot_general | solution.py:79
  141.9 4.1 convert_bitcast_fusion.2
  151.9 9.4 %bitcast_compare_fusion.4 = pred[8,1536,1024]{2,1,0:T(32,128)(4,1)} fusion(s32[1536]{0:T(1024)S(1)} %eq.177, s32[8,96,1024]{2,1,0:T(8,128)S(1)} %dynamic-slice_bitcast_fusion.14), kind=kLoop, calls=%fused_computation.9.clone.1 | loop fusion | flops 12582912 | bytes 15734784 | tf_op jit(solution)/shard_map/while/body/eval_jaxpr/eq | solution.py:54
  161.3 11.7 %bitcast_dynamic-update-slice_fusion.5 = (f32[4,8,64,1024]{3,2,1,0:T(8,128)}, f32[8,64,1024]{2,1,0:T(8,128)S(1)}) fusion(f32[4,8,64,1024]{3,2,1,0:T(8,128)} %get-tuple-element.383, s32[]{:T(128)} %get-tuple-element.382, bf16[8,64,1536]{1,2,0:T(8,128)(2,1)S(1)} %bitcast.165, pred[8,1536,1024]{2,1,0:T(32,128)(4,1)} %bitcast_compare_fusion.4), kind=kOutput, calls=%fused_computation.12.clone.1 | convolution fusion | flops 1610612736 | bytes 18350592 | tf_op jit(solution)/shard_map/while/body/eval_jaxpr/grk,gkl->grl/dot_general | solution.py:79
  174.3 4.1 convert_bitcast_fusion.2
  184.3 9.4 %bitcast_compare_fusion.4 = pred[8,1536,1024]{2,1,0:T(32,128)(4,1)} fusion(s32[1536]{0:T(1024)S(1)} %eq.177, s32[8,96,1024]{2,1,0:T(8,128)S(1)} %dynamic-slice_bitcast_fusion.14), kind=kLoop, calls=%fused_computation.9.clone.1 | loop fusion | flops 12582912 | bytes 15734784 | tf_op jit(solution)/shard_map/while/body/eval_jaxpr/eq | solution.py:54
  193.7 11.7 %bitcast_dynamic-update-slice_fusion.5 = (f32[4,8,64,1024]{3,2,1,0:T(8,128)}, f32[8,64,1024]{2,1,0:T(8,128)S(1)}) fusion(f32[4,8,64,1024]{3,2,1,0:T(8,128)} %get-tuple-element.383, s32[]{:T(128)} %get-tuple-element.382, bf16[8,64,1536]{1,2,0:T(8,128)(2,1)S(1)} %bitcast.165, pred[8,1536,1024]{2,1,0:T(32,128)(4,1)} %bitcast_compare_fusion.4), kind=kOutput, calls=%fused_computation.12.clone.1 | convolution fusion | flops 1610612736 | bytes 18350592 | tf_op jit(solution)/shard_map/while/body/eval_jaxpr/grk,gkl->grl/dot_general | solution.py:79
  206.7 4.1 convert_bitcast_fusion.2
  216.7 9.4 %bitcast_compare_fusion.4 = pred[8,1536,1024]{2,1,0:T(32,128)(4,1)} fusion(s32[1536]{0:T(1024)S(1)} %eq.177, s32[8,96,1024]{2,1,0:T(8,128)S(1)} %dynamic-slice_bitcast_fusion.14), kind=kLoop, calls=%fused_computation.9.clone.1 | loop fusion | flops 12582912 | bytes 15734784 | tf_op jit(solution)/shard_map/while/body/eval_jaxpr/eq | solution.py:54
  226.1 11.7 %bitcast_dynamic-update-slice_fusion.5 = (f32[4,8,64,1024]{3,2,1,0:T(8,128)}, f32[8,64,1024]{2,1,0:T(8,128)S(1)}) fusion(f32[4,8,64,1024]{3,2,1,0:T(8,128)} %get-tuple-element.383, s32[]{:T(128)} %get-tuple-element.382, bf16[8,64,1536]{1,2,0:T(8,128)(2,1)S(1)} %bitcast.165, pred[8,1536,1024]{2,1,0:T(32,128)(4,1)} %bitcast_compare_fusion.4), kind=kOutput, calls=%fused_computation.12.clone.1 | convolution fusion | flops 1610612736 | bytes 18350592 | tf_op jit(solution)/shard_map/while/body/eval_jaxpr/grk,gkl->grl/dot_general | solution.py:79
  242.3 11.5 %all_to_all.35 = f32[32,32,2]{0,2,1:T(2,128)S(1)} all-to-all(f32[32,32,2]{0,2,1:T(2,128)S(1)} %get-tuple-element.252), channel_id=1, replica_groups=mesh['corpus'=32,'query'=4] {'corpus'}, dimensions={1} | all-to-all | bytes 16384 | tf_op jit(solution)/shard_map/all_to_all | solution.py:188
  253.8 4.5 all-to-all-start.4
  259.8 6.2 gather_fusion
  267.0 6.2 gather_fusion.1
  273.7 4.5 scatter_custom_fusion.3
  279.6 7.5 %all-to-all-start.5 = ((f32[32,32,2]{0,2,1:T(2,128)}), f32[32,32,2]{0,2,1:T(2,128)S(1)}, u32[]{:S(2)}, u32[]{:S(2)}) async-start(f32[32,32,2]{0,2,1:T(2,128)} %copy.148), calls=%async_computation.5 | async-start | bytes 65536 | tf_op jit(solution)/shard_map/all_to_all | solution.py:217
  287.3 4.5 scatter_custom_fusion.2
  294.4 6.2 all-to-all-start.3
  302.1 5.8 all-to-all-done.3
  308.1 212.7 %while.28 = (s32[]{:T(128)}, f32[4,8,64,768]{3,1,0,2:T(8,128)}, f32[4,16,96,8]{1,3,2,0:T(8,128)}, s32[4,8,64,9]{2,1,3,0:T(8,128)S(1)}, f32[4,8,64,1024]{3,2,1,0:...) while((s32[]{:T(128)}, f32[4,8,64,768]{3,1,0,2:T(8,128)}, ...), condition=%wide.region_15.16_spmd.clone, body=%wide.region_13.15_spmd.clone.sunk | while | flops 1788871168 | bytes 67385192 | solution.py:129
  309.1 7.1 %select_reduce_fusion.2 = f32[8,64,1024]{2,1,0:T(8,128)} fusion(f32[8]{0:T(128)S(1)} %subtract_multiply_fusion.2, s32[8,64,8]{2,1,0:T(8,128)S(1)} %copy.187), kind=kLoop, calls=%fused_computation.21.clone.1 | loop fusion | flops 12058624 | bytes 2113568 | tf_op jit(solution)/shard_map/while/body/eval_jaxpr/reduce_sum | solution.py:112
  320.4 9.3 %bitcast_compare_fusion.5 = pred[8,1536,1024]{2,1,0:T(32,128)(4,1)} fusion(s32[1536]{0:T(1024)S(1)} %eq.184, s32[8,96,1024]{2,1,0:T(8,128)S(1)} %dynamic-slice_bitcast_fusion.15), kind=kLoop, calls=%fused_computation.19.clone.1 | loop fusion | flops 12582912 | bytes 15734784 | tf_op jit(solution)/shard_map/while/body/eval_jaxpr/eq | solution.py:54
  329.7 12.8 %fusion.84 = f32[8,64,1536]{1,2,0:T(8,128)} fusion(pred[8,1536,1024]{2,1,0:T(32,128)(4,1)} %bitcast_compare_fusion.5, f32[8,64,1024]{2,1,0:T(8,128)} %select_reduce_fusion.2, f32[4,8,64,1024]{3,2,1,0:T(8,128)} %get-tuple-element.426, s32[]{:T(128)} %get-tuple-element.411, f32[8,64]{1,0:T(8,128)S(1)} %get-tuple-element.371, ...), kind=kOutput, calls=%fused_computation.38.clone.1 | convolution fusion | flops 1613234176 | bytes 19928576 | tf_op jit(solution)/shard_map/while/body/eval_jaxpr/grl,gkl->grk/dot_general | solution.py:118
  342.6 5.5 fusion.85
  350.4 2.7 constant_dynamic-update-slice_fusion.2
  353.1 8.3 %fusion.86 = f32[4,16,96,8]{1,3,2,0:T(8,128)} fusion(f32[4,16,96,8]{1,3,2,0:T(8,128)} %get-tuple-element.413, s32[]{:T(128)} %get-tuple-element.411, f32[8,64,96,16]{1,3,2,0:T(8,128)} %bitcast.164, bf16[4,8,64,768]{2,3,1,0:T(8,128)(2,1)} %get-tuple-element.431), kind=kOutput, calls=%fused_computation.37.clone.1 | convolution fusion | flops 75497472 | bytes 8258560 | tf_op jit(solution)/shard_map/while/body/eval_jaxpr/grmk,grme->kme/dot_general | solution.py:126
  362.2 7.1 %select_reduce_fusion.2 = f32[8,64,1024]{2,1,0:T(8,128)} fusion(f32[8]{0:T(128)S(1)} %subtract_multiply_fusion.2, s32[8,64,8]{2,1,0:T(8,128)S(1)} %copy.187), kind=kLoop, calls=%fused_computation.21.clone.1 | loop fusion | flops 12058624 | bytes 2113568 | tf_op jit(solution)/shard_map/while/body/eval_jaxpr/reduce_sum | solution.py:112
  373.5 9.3 %bitcast_compare_fusion.5 = pred[8,1536,1024]{2,1,0:T(32,128)(4,1)} fusion(s32[1536]{0:T(1024)S(1)} %eq.184, s32[8,96,1024]{2,1,0:T(8,128)S(1)} %dynamic-slice_bitcast_fusion.15), kind=kLoop, calls=%fused_computation.19.clone.1 | loop fusion | flops 12582912 | bytes 15734784 | tf_op jit(solution)/shard_map/while/body/eval_jaxpr/eq | solution.py:54
  382.8 12.8 %fusion.84 = f32[8,64,1536]{1,2,0:T(8,128)} fusion(pred[8,1536,1024]{2,1,0:T(32,128)(4,1)} %bitcast_compare_fusion.5, f32[8,64,1024]{2,1,0:T(8,128)} %select_reduce_fusion.2, f32[4,8,64,1024]{3,2,1,0:T(8,128)} %get-tuple-element.426, s32[]{:T(128)} %get-tuple-element.411, f32[8,64]{1,0:T(8,128)S(1)} %get-tuple-element.371, ...), kind=kOutput, calls=%fused_computation.38.clone.1 | convolution fusion | flops 1613234176 | bytes 19928576 | tf_op jit(solution)/shard_map/while/body/eval_jaxpr/grl,gkl->grk/dot_general | solution.py:118
  395.6 5.5 fusion.85
  403.5 2.7 constant_dynamic-update-slice_fusion.2
  406.2 8.2 %fusion.86 = f32[4,16,96,8]{1,3,2,0:T(8,128)} fusion(f32[4,16,96,8]{1,3,2,0:T(8,128)} %get-tuple-element.413, s32[]{:T(128)} %get-tuple-element.411, f32[8,64,96,16]{1,3,2,0:T(8,128)} %bitcast.164, bf16[4,8,64,768]{2,3,1,0:T(8,128)(2,1)} %get-tuple-element.431), kind=kOutput, calls=%fused_computation.37.clone.1 | convolution fusion | flops 75497472 | bytes 8258560 | tf_op jit(solution)/shard_map/while/body/eval_jaxpr/grmk,grme->kme/dot_general | solution.py:126
  415.2 7.1 %select_reduce_fusion.2 = f32[8,64,1024]{2,1,0:T(8,128)} fusion(f32[8]{0:T(128)S(1)} %subtract_multiply_fusion.2, s32[8,64,8]{2,1,0:T(8,128)S(1)} %copy.187), kind=kLoop, calls=%fused_computation.21.clone.1 | loop fusion | flops 12058624 | bytes 2113568 | tf_op jit(solution)/shard_map/while/body/eval_jaxpr/reduce_sum | solution.py:112
  426.5 9.3 %bitcast_compare_fusion.5 = pred[8,1536,1024]{2,1,0:T(32,128)(4,1)} fusion(s32[1536]{0:T(1024)S(1)} %eq.184, s32[8,96,1024]{2,1,0:T(8,128)S(1)} %dynamic-slice_bitcast_fusion.15), kind=kLoop, calls=%fused_computation.19.clone.1 | loop fusion | flops 12582912 | bytes 15734784 | tf_op jit(solution)/shard_map/while/body/eval_jaxpr/eq | solution.py:54
  435.9 12.8 %fusion.84 = f32[8,64,1536]{1,2,0:T(8,128)} fusion(pred[8,1536,1024]{2,1,0:T(32,128)(4,1)} %bitcast_compare_fusion.5, f32[8,64,1024]{2,1,0:T(8,128)} %select_reduce_fusion.2, f32[4,8,64,1024]{3,2,1,0:T(8,128)} %get-tuple-element.426, s32[]{:T(128)} %get-tuple-element.411, f32[8,64]{1,0:T(8,128)S(1)} %get-tuple-element.371, ...), kind=kOutput, calls=%fused_computation.38.clone.1 | convolution fusion | flops 1613234176 | bytes 19928576 | tf_op jit(solution)/shard_map/while/body/eval_jaxpr/grl,gkl->grk/dot_general | solution.py:118
  448.7 5.5 fusion.85
  456.5 2.7 constant_dynamic-update-slice_fusion.2
  459.3 8.2 %fusion.86 = f32[4,16,96,8]{1,3,2,0:T(8,128)} fusion(f32[4,16,96,8]{1,3,2,0:T(8,128)} %get-tuple-element.413, s32[]{:T(128)} %get-tuple-element.411, f32[8,64,96,16]{1,3,2,0:T(8,128)} %bitcast.164, bf16[4,8,64,768]{2,3,1,0:T(8,128)(2,1)} %get-tuple-element.431), kind=kOutput, calls=%fused_computation.37.clone.1 | convolution fusion | flops 75497472 | bytes 8258560 | tf_op jit(solution)/shard_map/while/body/eval_jaxpr/grmk,grme->kme/dot_general | solution.py:126
  468.3 7.1 %select_reduce_fusion.2 = f32[8,64,1024]{2,1,0:T(8,128)} fusion(f32[8]{0:T(128)S(1)} %subtract_multiply_fusion.2, s32[8,64,8]{2,1,0:T(8,128)S(1)} %copy.187), kind=kLoop, calls=%fused_computation.21.clone.1 | loop fusion | flops 12058624 | bytes 2113568 | tf_op jit(solution)/shard_map/while/body/eval_jaxpr/reduce_sum | solution.py:112
  479.6 9.3 %bitcast_compare_fusion.5 = pred[8,1536,1024]{2,1,0:T(32,128)(4,1)} fusion(s32[1536]{0:T(1024)S(1)} %eq.184, s32[8,96,1024]{2,1,0:T(8,128)S(1)} %dynamic-slice_bitcast_fusion.15), kind=kLoop, calls=%fused_computation.19.clone.1 | loop fusion | flops 12582912 | bytes 15734784 | tf_op jit(solution)/shard_map/while/body/eval_jaxpr/eq | solution.py:54
  489.0 12.8 %fusion.84 = f32[8,64,1536]{1,2,0:T(8,128)} fusion(pred[8,1536,1024]{2,1,0:T(32,128)(4,1)} %bitcast_compare_fusion.5, f32[8,64,1024]{2,1,0:T(8,128)} %select_reduce_fusion.2, f32[4,8,64,1024]{3,2,1,0:T(8,128)} %get-tuple-element.426, s32[]{:T(128)} %get-tuple-element.411, f32[8,64]{1,0:T(8,128)S(1)} %get-tuple-element.371, ...), kind=kOutput, calls=%fused_computation.38.clone.1 | convolution fusion | flops 1613234176 | bytes 19928576 | tf_op jit(solution)/shard_map/while/body/eval_jaxpr/grl,gkl->grk/dot_general | solution.py:118
  501.8 5.5 fusion.85
  509.6 2.7 constant_dynamic-update-slice_fusion.2
  512.4 8.2 %fusion.86 = f32[4,16,96,8]{1,3,2,0:T(8,128)} fusion(f32[4,16,96,8]{1,3,2,0:T(8,128)} %get-tuple-element.413, s32[]{:T(128)} %get-tuple-element.411, f32[8,64,96,16]{1,3,2,0:T(8,128)} %bitcast.164, bf16[4,8,64,768]{2,3,1,0:T(8,128)(2,1)} %get-tuple-element.431), kind=kOutput, calls=%fused_computation.37.clone.1 | convolution fusion | flops 75497472 | bytes 8258560 | tf_op jit(solution)/shard_map/while/body/eval_jaxpr/grmk,grme->kme/dot_general | solution.py:126
  523.2 84.9 %all_to_all.36 = f32[32,32,2,768]{3,0,2,1:T(8,128)S(1)} all-to-all(f32[32,32,2,768]{3,0,2,1:T(8,128)} %bitcast.170), channel_id=1, replica_groups=mesh['corpus'=32,'query'=4] {'corpus'}, dimensions={1} | all-to-all | bytes 12582912 | tf_op jit(solution)/shard_map/all_to_all | solution.py:232
  608.0 7.5 %copy.154 = f32[32,32,2,768]{3,2,1,0:T(2,128)} copy(f32[32,32,2,768]{3,0,2,1:T(8,128)S(1)} %all_to_all.36) | data formatting | bytes 12582912 | tf_op jit(solution)/shard_map/all_to_all | solution.py:232
  615.5 8.5 %reshape.318 = f32[2048,768]{1,0:T(8,128)} reshape(f32[32,32,2,768]{3,2,1,0:T(2,128)} %copy.154) | data formatting | bytes 12582912 | tf_op jit(solution)/shard_map/reshape | solution.py:239
  624.0 8.7 %gather_fusion.2 = f32[1024,768]{1,0:T(8,128)} fusion(f32[2048,768]{1,0:T(8,128)} %reshape.318, s32[1024]{0:T(1024)S(1)} %copy-done.13), kind=kCustom, calls=%fused_computation.2 | custom fusion | bytes 6295552 | tf_op jit(solution)/shard_map/gather | solution.py:239
  632.7 3.1 reshape.319
  635.8 2.9 reduce_sum.74
  638.6 3.1 reduce_sum.76
  (227 shorter events, 94.5 us)
Async XLA Ops:
  8.9 1.9 copy-start.1
  16.0 0.8 copy-start.15
  16.8 16.1 %copy-start.6 = (bf16[256,768]{1,0:T(8,128)(2,1)S(1)}, bf16[256,768]{1,0:T(8,128)(2,1)}, u32[]{:S(2)}) copy-start(bf16[256,768]{1,0:T(8,128)(2,1)} %param.9) | copy-start | bytes 1179652
  17.5 17.1 %copy-start.14 = (s32[1024,1]{0,1:T(1,128)}, s32[1024,1]{0,1:T(1,128)S(1)}, u32[]{:S(2)}) copy-start(s32[1024,1]{0,1:T(1,128)S(1)} %compare_select_fusion.1) | copy-start | bytes 12292
  23.2 28.0 %all-to-all-start = ((s32[32,1,576]{2,1,0:T(1,128)}), s32[32,1,576]{2,1,0:T(1,128)S(1)}, u32[]{:S(2)}, u32[]{:S(2)}) async-start(s32[32,1,576]{2,1,0:T(1,128)} %reshape.389), calls=%async_computation | async-start | bytes 163840 | tf_op jit(solution)/shard_map/all_to_all | solution.py:173
  51.2 7.8 %copy-start.7 = (s32[32,1,576]{2,1,0:T(1,128)}, s32[32,1,576]{2,1,0:T(1,128)S(1)}, u32[]{:S(2)}) copy-start(s32[32,1,576]{2,1,0:T(1,128)S(1)} %all-to-all-done) | copy-start | bytes 221188
  51.2 47.3 %all-to-all-start.1 = ((bf16[32,32,2,768]{3,2,0,1:T(2,128)(2,1)}), bf16[32,32,2,768]{3,2,0,1:T(2,128)(2,1)S(1)}, u32[]{:S(2)}, u32[]{:S(2)}) async-start(bf16[32,32,2,768]{3,2,0,1:T(2,128)(2,1)} %copy.136), calls=%async_computation.1 | async-start | bytes 6291456 | tf_op jit(solution)/shard_map/all_to_all | solution.py:166
  65.7 0.7 copy-start.2
  119.5 9.4 %copy-start = (bf16[8,64,96,16]{1,3,2,0:T(8,128)(2,1)S(1)}, bf16[8,64,96,16]{1,3,2,0:T(8,128)(2,1)}, u32[]{:S(2)}) copy-start(bf16[8,64,96,16]{1,3,2,0:T(8,128)(2,1)} %copy.185) | copy-start | bytes 4718596 | tf_op jit(solution)/shard_map/while
  151.9 9.4 %copy-start = (bf16[8,64,96,16]{1,3,2,0:T(8,128)(2,1)S(1)}, bf16[8,64,96,16]{1,3,2,0:T(8,128)(2,1)}, u32[]{:S(2)}) copy-start(bf16[8,64,96,16]{1,3,2,0:T(8,128)(2,1)} %copy.185) | copy-start | bytes 4718596 | tf_op jit(solution)/shard_map/while
  184.3 9.4 %copy-start = (bf16[8,64,96,16]{1,3,2,0:T(8,128)(2,1)S(1)}, bf16[8,64,96,16]{1,3,2,0:T(8,128)(2,1)}, u32[]{:S(2)}) copy-start(bf16[8,64,96,16]{1,3,2,0:T(8,128)(2,1)} %copy.185) | copy-start | bytes 4718596 | tf_op jit(solution)/shard_map/while
  216.7 9.4 %copy-start = (bf16[8,64,96,16]{1,3,2,0:T(8,128)(2,1)S(1)}, bf16[8,64,96,16]{1,3,2,0:T(8,128)(2,1)}, u32[]{:S(2)}) copy-start(bf16[8,64,96,16]{1,3,2,0:T(8,128)(2,1)} %copy.185) | copy-start | bytes 4718596 | tf_op jit(solution)/shard_map/while
  253.8 12.4 %all-to-all-start.4 = ((f32[32,32,2]{0,2,1:T(2,128)}), f32[32,32,2]{0,2,1:T(2,128)S(1)}, u32[]{:S(2)}, u32[]{:S(2)}) async-start(f32[32,32,2]{0,2,1:T(2,128)} %get-tuple-element.251), calls=%async_computation.4 | async-start | bytes 65536 | tf_op jit(solution)/shard_map/all_to_all | solution.py:195
  259.0 14.2 %copy-start.12 = (s32[1024]{0:T(1024)}, s32[1024]{0:T(1024)S(1)}, u32[]{:S(2)}) copy-start(s32[1024]{0:T(1024)S(1)} %broadcast_clamp_fusion) | copy-start | bytes 12292
  266.2 34.6 %copy-start.3 = (s32[32,32,2,9]{0,2,1,3:T(2,128)S(1)}, s32[32,32,2,9]{0,2,1,3:T(2,128)}, u32[]{:S(2)}) copy-start(s32[32,32,2,9]{0,2,1,3:T(2,128)} %copy-done.2) | copy-start | bytes 221188
  279.6 14.8 %all-to-all-start.5 = ((f32[32,32,2]{0,2,1:T(2,128)}), f32[32,32,2]{0,2,1:T(2,128)S(1)}, u32[]{:S(2)}, u32[]{:S(2)}) async-start(f32[32,32,2]{0,2,1:T(2,128)} %copy.148), calls=%async_computation.5 | async-start | bytes 65536 | tf_op jit(solution)/shard_map/all_to_all | solution.py:217
  294.4 13.5 %all-to-all-start.3 = ((f32[32,32,2]{0,2,1:T(2,128)}), f32[32,32,2]{0,2,1:T(2,128)S(1)}, u32[]{:S(2)}, u32[]{:S(2)}) async-start(f32[32,32,2]{0,2,1:T(2,128)} %copy.144), calls=%async_computation.3 | async-start | bytes 65536 | tf_op jit(solution)/shard_map/all_to_all | solution.py:210
  300.6 338.0 %all-gather.2.cloned.1.call-start = ((), (), s32[]{:S(2)}) async-start(), calls=%async_computation.7 | async-start | bytes 6340608 | tf_op jit(solution)/shard_map/all_gather | solution.py:241
  308.3 0.6 copy-start.8
  308.3 0.6 copy-start.10
  308.3 8.5 %copy-start.4 = (s32[4,8,64,9]{2,1,3,0:T(8,128)}, s32[4,8,64,9]{2,1,3,0:T(8,128)S(1)}, u32[]{:S(2)}) copy-start(s32[4,8,64,9]{2,1,3,0:T(8,128)S(1)} %get-tuple-element.425) | copy-start | bytes 221188 | tf_op jit(solution)/shard_map/while
  353.1 8.3 %copy-start.5 = (s32[4,8,64,9]{2,1,3,0:T(8,128)S(1)}, s32[4,8,64,9]{2,1,3,0:T(8,128)}, u32[]{:S(2)}) copy-start(s32[4,8,64,9]{2,1,3,0:T(8,128)} %copy-done.4) | copy-start | bytes 221188 | tf_op jit(solution)/shard_map/while
  353.1 8.3 %copy-start.9 = (f32[4,8,64]{2,1,0:T(8,128)S(1)}, f32[4,8,64]{2,1,0:T(8,128)}, u32[]{:S(2)}) copy-start(f32[4,8,64]{2,1,0:T(8,128)} %copy-done.8) | copy-start | bytes 24580 | tf_op jit(solution)/shard_map/while
  353.1 8.3 %copy-start.11 = (f32[4,8,64]{2,1,0:T(8,128)S(1)}, f32[4,8,64]{2,1,0:T(8,128)}, u32[]{:S(2)}) copy-start(f32[4,8,64]{2,1,0:T(8,128)} %copy-done.10) | copy-start | bytes 24580 | tf_op jit(solution)/shard_map/while
  361.4 0.6 copy-start.8
  361.4 0.6 copy-start.10
  361.4 8.5 %copy-start.4 = (s32[4,8,64,9]{2,1,3,0:T(8,128)}, s32[4,8,64,9]{2,1,3,0:T(8,128)S(1)}, u32[]{:S(2)}) copy-start(s32[4,8,64,9]{2,1,3,0:T(8,128)S(1)} %get-tuple-element.425) | copy-start | bytes 221188 | tf_op jit(solution)/shard_map/while
  406.2 8.2 %copy-start.5 = (s32[4,8,64,9]{2,1,3,0:T(8,128)S(1)}, s32[4,8,64,9]{2,1,3,0:T(8,128)}, u32[]{:S(2)}) copy-start(s32[4,8,64,9]{2,1,3,0:T(8,128)} %copy-done.4) | copy-start | bytes 221188 | tf_op jit(solution)/shard_map/while
  406.2 8.2 %copy-start.9 = (f32[4,8,64]{2,1,0:T(8,128)S(1)}, f32[4,8,64]{2,1,0:T(8,128)}, u32[]{:S(2)}) copy-start(f32[4,8,64]{2,1,0:T(8,128)} %copy-done.8) | copy-start | bytes 24580 | tf_op jit(solution)/shard_map/while
  406.2 8.2 %copy-start.11 = (f32[4,8,64]{2,1,0:T(8,128)S(1)}, f32[4,8,64]{2,1,0:T(8,128)}, u32[]{:S(2)}) copy-start(f32[4,8,64]{2,1,0:T(8,128)} %copy-done.10) | copy-start | bytes 24580 | tf_op jit(solution)/shard_map/while
  414.4 0.6 copy-start.8
  414.5 0.6 copy-start.10
  414.5 8.5 %copy-start.4 = (s32[4,8,64,9]{2,1,3,0:T(8,128)}, s32[4,8,64,9]{2,1,3,0:T(8,128)S(1)}, u32[]{:S(2)}) copy-start(s32[4,8,64,9]{2,1,3,0:T(8,128)S(1)} %get-tuple-element.425) | copy-start | bytes 221188 | tf_op jit(solution)/shard_map/while
  459.3 8.3 %copy-start.5 = (s32[4,8,64,9]{2,1,3,0:T(8,128)S(1)}, s32[4,8,64,9]{2,1,3,0:T(8,128)}, u32[]{:S(2)}) copy-start(s32[4,8,64,9]{2,1,3,0:T(8,128)} %copy-done.4) | copy-start | bytes 221188 | tf_op jit(solution)/shard_map/while
  459.3 8.3 %copy-start.9 = (f32[4,8,64]{2,1,0:T(8,128)S(1)}, f32[4,8,64]{2,1,0:T(8,128)}, u32[]{:S(2)}) copy-start(f32[4,8,64]{2,1,0:T(8,128)} %copy-done.8) | copy-start | bytes 24580 | tf_op jit(solution)/shard_map/while
  459.3 8.3 %copy-start.11 = (f32[4,8,64]{2,1,0:T(8,128)S(1)}, f32[4,8,64]{2,1,0:T(8,128)}, u32[]{:S(2)}) copy-start(f32[4,8,64]{2,1,0:T(8,128)} %copy-done.10) | copy-start | bytes 24580 | tf_op jit(solution)/shard_map/while
  467.5 0.6 copy-start.8
  467.5 0.6 copy-start.10
  467.5 8.5 %copy-start.4 = (s32[4,8,64,9]{2,1,3,0:T(8,128)}, s32[4,8,64,9]{2,1,3,0:T(8,128)S(1)}, u32[]{:S(2)}) copy-start(s32[4,8,64,9]{2,1,3,0:T(8,128)S(1)} %get-tuple-element.425) | copy-start | bytes 221188 | tf_op jit(solution)/shard_map/while
  512.4 8.2 %copy-start.5 = (s32[4,8,64,9]{2,1,3,0:T(8,128)S(1)}, s32[4,8,64,9]{2,1,3,0:T(8,128)}, u32[]{:S(2)}) copy-start(s32[4,8,64,9]{2,1,3,0:T(8,128)} %copy-done.4) | copy-start | bytes 221188 | tf_op jit(solution)/shard_map/while
  512.4 8.2 %copy-start.9 = (f32[4,8,64]{2,1,0:T(8,128)S(1)}, f32[4,8,64]{2,1,0:T(8,128)}, u32[]{:S(2)}) copy-start(f32[4,8,64]{2,1,0:T(8,128)} %copy-done.8) | copy-start | bytes 24580 | tf_op jit(solution)/shard_map/while
  512.4 8.2 %copy-start.11 = (f32[4,8,64]{2,1,0:T(8,128)S(1)}, f32[4,8,64]{2,1,0:T(8,128)}, u32[]{:S(2)}) copy-start(f32[4,8,64]{2,1,0:T(8,128)} %copy-done.10) | copy-start | bytes 24580 | tf_op jit(solution)/shard_map/while
  615.5 8.5 %copy-start.13 = (s32[1024]{0:T(1024)S(1)}, s32[1024]{0:T(1024)}, u32[]{:S(2)}) copy-start(s32[1024]{0:T(1024)} %copy-done.12) | copy-start | bytes 12292
Sparse Core Ops, SparseCore 0:
  523.3 90.4 all-gather.1
